TPU v7x, 32 devices: a whole 2x2x4 slice. The times are simulated.
32 devices in a mesh: seg: 16 (over z, x, core), blk: 2 (over y).
Axes of the slice: x: 2, y: 2, z: 4, core: 2. Of those that a mesh axis runs over, the one named last changes fastest.
Arguments:
- queries: bfloat16 [4096, 2048], P(('seg', 'blk')), may hold values from -6 to 6
- keys: bfloat16 [4096, 2048], P(('seg', 'blk')), may hold values from -6 to 6
- values: bfloat16 [4096, 2048], P(('seg', 'blk')), may hold values from -6 to 6
- mid_offset: int32 [16], replicated, may hold values from 0 to 15, as said below
- far_offset: int32 [16], replicated, may hold values from 0 to 127, as said below
Outputs:
- attended: bfloat16 [4096, 2048], P(('seg', 'blk'))
Inputs may be any that keep to these rules, and one draw needn't show every extreme that they name: `mid_offset`: one head has offset 0 and another 16 - 1. `far_offset`: one head has offset 0 and another 128 - 1.
All inputs are finite; a program needn't handle non-finite values.
Results may differ from a plain program's by a relative error of at most 0.0065.
Values may be sent and summed in bfloat16 or wider, within the bound.
A program may use at most 64 MiB of HBM per device.

v0:
```python
import math
import jax
import jax.numpy as jnp
from jax import lax
from jax.sharding import PartitionSpec as P

HEADS = 16
DH = 128
SPAN = 4
MID_RATE = 16
very_low = -1e30


def from_partner(shard, axis, bit):
    return lax.ppermute(shard, axis, [(i, i ^ 1 << bit) for i in range(lax.axis_size(axis))])


def attend_direct(query_rows, key_rows, value_rows):
    score_scale = 1.0 / math.sqrt(query_rows.shape[-1])
    scores = (
        jnp.einsum("qhd,khd->hqk", query_rows, key_rows, preferred_element_type=jnp.float32)
        * score_scale
    )
    row_top = jnp.max(scores, axis=-1)
    weights = jnp.exp(scores - row_top[..., None])
    totals = jnp.sum(weights, axis=-1)
    mixed = jnp.einsum(
        "hqk,khd->qhd", weights.astype(jnp.bfloat16), value_rows, preferred_element_type=jnp.float32
    )
    return (mixed / jnp.transpose(totals)[..., None], jnp.transpose(row_top + jnp.log(totals)))


def online_start(heads, rows, dims):
    return (
        jnp.full((heads, rows), very_low, jnp.float32),
        jnp.zeros((heads, rows), jnp.float32),
        jnp.zeros((heads, rows, dims), jnp.float32),
    )


def online_step(state_now, query_rows, key_rows, value_rows):
    row_top, totals, mixed = state_now
    score_scale = 1.0 / math.sqrt(query_rows.shape[-1])
    scores = (
        jnp.einsum("qhd,khd->hqk", query_rows, key_rows, preferred_element_type=jnp.float32)
        * score_scale
    )
    new_top = jnp.maximum(row_top, jnp.max(scores, axis=-1))
    weights = jnp.exp(scores - new_top[..., None])
    totals = jnp.sum(weights, axis=-1)
    mixed = jnp.einsum(
        "hqk,khd->hqd", weights.astype(jnp.bfloat16), value_rows, preferred_element_type=jnp.float32
    )
    return (new_top, totals, mixed)


def online_finish(state_now):
    row_top, totals, mixed = state_now
    level_out = jnp.transpose(mixed / totals[..., None], (1, 0, 2))
    return (level_out, jnp.transpose(row_top + jnp.log(totals)))


def combine_levels(
    dense_out, dense_lse, mid_out, mid_lse, far_out, far_lse, mid_offset, far_offset
):
    rows = dense_out.shape[0]
    heads = dense_out.shape[1]
    dims = dense_out.shape[2]
    rate = rows // mid_out.shape[0]
    mid_hit = jnp.arange(rate, dtype=jnp.int32)[:, None] == mid_offset[None, :]
    mid_full = jnp.where(mid_hit[None, :, :, None], mid_out[:, None], 0.0).reshape(
        rows, heads, dims
    )
    mid_lse_full = jnp.where(mid_hit[None], mid_lse[:, None, :], very_low).reshape(rows, heads)
    far_hit = jnp.arange(rows, dtype=jnp.int32)[:, None] == far_offset[None, :]
    far_full = jnp.where(far_hit[..., None], far_out[None], 0.0)
    far_lse_full = jnp.where(far_hit, far_lse[None], very_low)
    level_top = jnp.maximum(dense_lse, jnp.maximum(mid_lse_full, far_lse_full))
    dense_weight = jnp.exp(dense_lse - level_top)
    mid_weight = jnp.exp(mid_lse_full - level_top)
    far_weight = jnp.exp(far_lse_full - level_top)
    mixed = (
        dense_weight[..., None] * dense_out
        + mid_weight[..., None] * mid_full
        + far_weight[..., None] * far_full
    )
    mixed = mixed / (dense_weight + mid_weight + far_weight)[..., None]
    return mixed.astype(jnp.bfloat16).reshape(rows, heads * dims)


def on_device(queries, keys, values, mid_offset, far_offset):
    rows = queries.shape[0]
    query_rows = queries.reshape(rows, HEADS, DH)
    key_rows = keys.reshape(rows, HEADS, DH)
    value_rows = values.reshape(rows, HEADS, DH)
    piece_rows = (
        lax.all_gather(keys, "blk", axis=0, tiled=True),
        lax.all_gather(values, "blk", axis=0, tiled=True),
    )
    key_piece = piece_rows[0].reshape(-1, HEADS, DH)
    value_piece = piece_rows[1].reshape(-1, HEADS, DH)
    dense_state = online_step(online_start(HEADS, rows, DH), query_rows, key_piece, value_piece)
    dense_out, dense_lse = online_finish(dense_state)
    mid_select = (jnp.arange(MID_RATE, dtype=jnp.int32)[:, None] == mid_offset[None, :]).astype(
        jnp.bfloat16
    )

    def pick_mid(field):
        shaped = field.reshape(rows // MID_RATE, MID_RATE, HEADS, DH)
        return jnp.einsum(
            "jrhd,rh->jhd", shaped, mid_select, preferred_element_type=jnp.float32
        ).astype(jnp.bfloat16)

    mid_pairs = jnp.stack([pick_mid(key_rows), pick_mid(value_rows)])
    bit_count = SPAN.bit_length() - 1
    mid_pairs = lax.all_gather(mid_pairs, "blk", axis=1, tiled=True)
    for bit_index in range(bit_count):
        partner_rows = from_partner(mid_pairs, "seg", bit_index)
        mid_pairs = jnp.concatenate([mid_pairs, partner_rows], axis=1)
    mid_out, mid_lse = attend_direct(pick_mid(query_rows), mid_pairs[0], mid_pairs[1])
    far_select = (jnp.arange(rows, dtype=jnp.int32)[:, None] == far_offset[None, :]).astype(
        jnp.bfloat16
    )

    def pick_far(field):
        return jnp.einsum(
            "thd,th->hd", field, far_select, preferred_element_type=jnp.float32
        ).astype(jnp.bfloat16)[None]

    far_pairs = jnp.stack([pick_far(key_rows), pick_far(value_rows)])
    far_query = pick_far(query_rows)
    piece_rows = lax.all_gather(far_pairs, ("seg", "blk"), axis=1, tiled=True)
    far_state = online_step(online_start(HEADS, 1, DH), far_query, piece_rows[0], piece_rows[1])
    far_out, far_lse = online_finish(far_state)
    return combine_levels(
        dense_out, dense_lse, mid_out, mid_lse, far_out[0], far_lse[0], mid_offset, far_offset
    )


def solution(mesh):
    return jax.shard_map(
        on_device,
        mesh=mesh,
        in_specs=(
            P(("seg", "blk"), None),
            P(("seg", "blk"), None),
            P(("seg", "blk"), None),
            P(),
            P(),
        ),
        out_specs=P(("seg", "blk"), None),
        check_vma=False,
    )
```

profile of v0, /device:TPU:0, one launch (start us, length us, event | category | flops | bytes accessed | tf_op | source)
XLA Modules:
  0.0 114.1 jit_solution(16395666675392113394)
XLA Ops:
  6.5 2.1 %copy.17 = bf16[128,2048]{0,1:T(8,128)(2,1)} copy(bf16[128,2048]{1,0:T(8,128)(2,1)} %param.6) | data formatting | bytes 1048576 | tf_op args[1]
  8.7 1.2 %copy.49 = bf16[16,8,16,128]{3,2,1,0:T(8,128)(2,1)S(1)} copy(bf16[16,8,16,128]{3,1,2,0:T(8,128)(2,1)} %bitcast.150) | data formatting | bytes 1048576
  10.0 0.1 copy.48
  10.1 0.1 iota_compare_fusion.1
  10.2 0.2 fusion.22
  10.4 0.2 fusion.24
  10.7 5.9 %all_gather.13 = bf16[2,16,16,128]{3,1,2,0:T(8,128)(2,1)S(1)} all-gather(bf16[2,8,16,128]{3,1,2,0:T(8,128)(2,1)S(1)} %pad_maximum_fusion.1), channel_id=1, replica_groups=mesh['seg'=16,'blk'=2] {'blk'}, dimensions={1}, use_global_device_ids=true | all-gather | bytes 196608 | tf_op jit(solution)/shard_map/all_gather | solution.py:116
  16.7 0.2 fusion.12
  16.9 0.3 fusion.15
  17.2 0.3 fusion.18
  17.4 0.1 copy.47
  17.6 0.2 fusion.26
  17.8 71.3 %all_gather.14 = bf16[2,32,16,128]{3,2,1,0:T(8,128)(2,1)S(1)} all-gather(bf16[2,1,16,128]{3,2,1,0:T(8,128)(2,1)S(1)} %pad_maximum_fusion.2), channel_id=1, replica_groups=mesh['seg'=16,'blk'=2] {'seg','blk'}, dimensions={1}, use_global_device_ids=true | all-gather | bytes 270336 | tf_op jit(solution)/shard_map/all_gather | solution.py:132
  89.2 0.2 fusion.32
  89.4 0.1 multiply_reduce_fusion.1
  89.5 0.2 fusion.53
  89.7 0.2 fusion.30
  89.8 0.1 broadcast_divide_fusion
  90.1 0.1 broadcast_in_dim.103
  90.2 6.2 %collective-permute-done.1 = bf16[2,32,16,128]{3,1,2,0:T(8,128)(2,1)S(1)} collective-permute-done((bf16[2,32,16,128]{3,1,2,0:T(8,128)(2,1)S(1)}, bf16[2,32,16,128]{3,1,2,0:T(8,128)(2,1)S(1)}, u32[]{:S(2)}, u32[]{:S(2)}) %collective-permute-start.1) | collective-permute-done | bytes 262176 | tf_op jit(solution)/shard_map/ppermute | solution.py:15
  96.4 0.3 fusion.57
  96.7 0.2 fusion.35
  96.9 0.2 fusion.6
  97.2 0.1 broadcast_in_dim.109
  97.3 1.4 %copy.22 = f32[128,16,128]{0,2,1:T(8,128)} copy(f32[128,16,128]{2,1,0:T(8,128)S(1)} %bitcast.147) | data formatting | bytes 2097152 | tf_op jit(solution)/shard_map/jit(_where)/broadcast_in_dim | solution.py:71
  98.8 0.1 broadcast_in_dim.105
  98.9 1.7 %multiply_reduce_fusion = (f32[16,128]{1,0:T(8,128)S(1)}, f32[16,128,256]{2,1,0:T(8,128)S(1)}) fusion(bf16[256,16,128]{0,2,1:T(8,128)(2,1)} %bitcast.154, bf16[128,2048]{1,0:T(8,128)(2,1)S(1)} %copy-done), kind=kOutput, calls=%fused_computation.1 | convolution fusion | flops 135264256 | bytes 3678208 | tf_op jit(solution)/shard_map/qhd,khd->hqk/dot_general | solution.py:45
  100.7 0.7 fusion.1
  101.4 0.1 add_add_fusion
  101.5 2.3 %copy.20 = bf16[256,2048]{0,1:T(8,128)(2,1)} copy(bf16[256,2048]{1,0:T(8,128)(2,1)} %all-gather.5.cloned.1.call-done) | data formatting | bytes 2097152 | tf_op jit(solution)/shard_map/all_gather | solution.py:98
  103.8 2.4 %divide_convert_fusion = bf16[128,16,128]{0,2,1:T(8,128)(2,1)S(1)} fusion(f32[128,16,128]{0,2,1:T(8,128)} %copy.22, bf16[256,16,128]{0,2,1:T(8,128)(2,1)} %bitcast.155, f32[16,128,256]{2,1,0:T(8,128)S(1)} %get-tuple-element.20, f32[16,128]{1,0:T(8,128)S(1)} %broadcast_maximum_fusion, f32[128,16]{0,1:T(8,128)S(1)} %get-tuple-element.5, ...), kind=kOutput, calls=%fused_computation.12 | convolution fusion | flops 138412032 | bytes 4780032 | tf_op jit(solution)/shard_map/hqk,khd->hqd/dot_general | solution.py:51
  106.2 1.0 copy.23
  (37 shorter events, 0.6 us)
Async XLA Ops:
  6.5 3.4 %copy-start.1 = (bf16[128,2048]{1,0:T(8,128)(2,1)S(1)}, bf16[128,2048]{1,0:T(8,128)(2,1)}, u32[]{:S(2)}) copy-start(bf16[128,2048]{1,0:T(8,128)(2,1)} %param.6) | copy-start | bytes 1572868
  6.5 3.6 %copy-start.4 = (s32[16]{0:T(128)S(1)}, s32[16]{0:T(128)}, u32[]{:S(2)}) copy-start(s32[16]{0:T(128)} %param.8) | copy-start | bytes 196
  6.5 92.4 %all-gather.3.cloned.1.call-start = ((), (), s32[]{:S(2)}) async-start(), calls=%async_computation | async-start | bytes 1572864 | tf_op jit(solution)/shard_map/all_gather | solution.py:97
  8.7 92.8 %all-gather.5.cloned.1.call-start = ((), (), s32[]{:S(2)}) async-start(), calls=%async_computation.1 | async-start | bytes 1572864 | tf_op jit(solution)/shard_map/all_gather | solution.py:98
  8.7 7.9 %copy-start.3 = (s32[16]{0:T(128)S(1)}, s32[16]{0:T(128)}, u32[]{:S(2)}) copy-start(s32[16]{0:T(128)} %param.9) | copy-start | bytes 196
  8.7 8.0 %copy-start.2 = (bf16[128,2048]{1,0:T(8,128)(2,1)S(1)}, bf16[128,2048]{1,0:T(8,128)(2,1)}, u32[]{:S(2)}) copy-start(bf16[128,2048]{1,0:T(8,128)(2,1)} %param.7) | copy-start | bytes 1572868
  10.0 7.2 %copy-start = (bf16[128,2048]{1,0:T(8,128)(2,1)S(1)}, bf16[128,2048]{1,0:T(8,128)(2,1)}, u32[]{:S(2)}) copy-start(bf16[128,2048]{1,0:T(8,128)(2,1)} %param.5) | copy-start | bytes 1572868
  16.6 73.3 %collective-permute-start = (bf16[2,16,16,128]{3,1,2,0:T(8,128)(2,1)S(1)}, bf16[2,16,16,128]{3,1,2,0:T(8,128)(2,1)S(1)}, u32[]{:S(2)}, u32[]{:S(2)}) collective-permute-start(bf16[2,16,16,128]{3,1,2,0:T(8,128)(2,1)S(1)} %all_gather.13), channel_id=1, source_target_pairs={{0,2},{2,0},{4,6},{6,4},{8,10},{10,8},{12,14},{14,12},{16,18},{18,... | collective-permute-start | bytes 393224 | tf_op jit(solution)/shard_map/ppermute | solution.py:15
  90.0 6.4 %collective-permute-start.1 = (bf16[2,32,16,128]{3,1,2,0:T(8,128)(2,1)S(1)}, bf16[2,32,16,128]{3,1,2,0:T(8,128)(2,1)S(1)}, u32[]{:S(2)}, u32[]{:S(2)}) collective-permute-start(bf16[2,32,16,128]{3,1,2,0:T(8,128)(2,1)S(1)} %pad_maximum_fusion), channel_id=1, source_target_pairs={{0,4},{2,6},{4,0},{6,2},{8,12},{10,14},{12,8},{14,10},{16,20},{18,... | collective-permute-start | bytes 786440 | tf_op jit(solution)/shard_map/ppermute | solution.py:15
Sparse Core Ops, SparseCore 0:
  8.9 24.9 all-gather.2
  35.4 22.6 all-gather.4
where the time goes:
time: 114 us
  blocking collectives  77.2 us (68%)
  between operations  13.7 us (12%)
  local copies, waits for them, and re-layouts  8.74 us (8%)
  matrix products  6.45 us (6%)
  waiting for transfers between devices  6.26 us (5%)
  other arithmetic  1.62 us (1%)
    all_gather x1, blocking collectives, on_device(): piece_rows = lax.all_gather(far_pairs, ('seg', 'blk'), axis=1, tiled=True)  71.3 us
    ppermute x2, waiting for transfers between devices, from_partner(): lax.ppermute(shard, axis, [(i, i ^ 1 << bit) for i in range(lax.axis_size...  6.19 us
    all_gather x1, blocking collectives, on_device(): mid_pairs = lax.all_gather(mid_pairs, 'blk', axis=1, tiled=True)  5.89 us
    unnamed x16, local copies, waits for them, and re-layouts  3.61 us
    dot_general x2, matrix products, online_step(): jnp.einsum('hqk,khd->hqd', weights.astype(jnp.bfloat16), value_rows, pref...  2.59 us
  transfers between devices with their start and end apart: 4, of which 1 were waited for; matrix products, arithmetic and copies ran while one was open for 8% of the time, Pallas kernels for 0%

commit v1 on v0

--- a/solution.py
+++ b/solution.py
@@ -93,9 +93,23 @@
     query_rows = queries.reshape(rows, HEADS, DH)
     key_rows = keys.reshape(rows, HEADS, DH)
     value_rows = values.reshape(rows, HEADS, DH)
+
+    def _expand_patches(unit, shard_axis):
+        x_new, top = (lax.psum(1, shard_axis), lax.axis_index(shard_axis))
+        k_now, frame_out = (unit, 1)
+        while frame_out < x_new:
+            piece_out = lax.ppermute(
+                k_now, shard_axis, list(map(lambda b: (b, b ^ frame_out), range(x_new)))
+            )
+            big = jnp.concatenate([k_now, piece_out], 0)
+            outer = jnp.concatenate([piece_out, k_now], 0)
+            k_now = jnp.where(top & frame_out == 0, big, outer)
+            frame_out = 2 * frame_out
+        return k_now
+
     piece_rows = (
         lax.all_gather(keys, "blk", axis=0, tiled=True),
-        lax.all_gather(values, "blk", axis=0, tiled=True),
+        _expand_patches(values, shard_axis="blk"),
     )
     key_piece = piece_rows[0].reshape(-1, HEADS, DH)
     value_piece = piece_rows[1].reshape(-1, HEADS, DH)

time: 114 us -> 118 us (1.035)
  blocking collectives: 77.2 us -> 80.6 us
  starting transfers between devices: 0.12 us -> 3.04 us
  local copies, waits for them, and re-layouts: 8.74 us -> 6.94 us
    all_gather x1, blocking collectives: 5.89 us -> 9.93 us  [on_device(): mid_pairs = lax.all_gather(mid_pairs, 'blk', axis=1, tiled=True)]
    ppermute x0 -> x1, starting transfers between devices: none -> 2.97 us  [_expand_patches(): lax.ppermute(k_now, shard_axis, list(map(lambda b: (b, b ^ frame_out), ra...]
    all_gather x1 -> x0, local copies, waits for them, and re-layouts: 2.28 us -> none  [on_device(): lax.all_gather(values, 'blk', axis=0, tiled=True)]
    dot_general x2, matrix products: 2.59 us -> 1.26 us  [online_step(): jnp.einsum('hqk,khd->hqd', weights.astype(jnp.bfloat16), value_rows, pref...]
where the time goes in v1:
time: 118 us
  blocking collectives  80.6 us (68%)
  between operations  13.7 us (12%)
  local copies, waits for them, and re-layouts  6.94 us (6%)
  waiting for transfers between devices  6.22 us (5%)
  matrix products  5.33 us (5%)
  starting transfers between devices  3.04 us (3%)
  other arithmetic  2.3 us (2%)
    all_gather x1, blocking collectives, on_device(): piece_rows = lax.all_gather(far_pairs, ('seg', 'blk'), axis=1, tiled=True)  70.7 us
    all_gather x1, blocking collectives, on_device(): mid_pairs = lax.all_gather(mid_pairs, 'blk', axis=1, tiled=True)  9.93 us
    ppermute x2, waiting for transfers between devices, from_partner(): lax.ppermute(shard, axis, [(i, i ^ 1 << bit) for i in range(lax.axis_size...  6.18 us
    unnamed x16, local copies, waits for them, and re-layouts  3.53 us
    ppermute x1, starting transfers between devices, _expand_patches(): lax.ppermute(k_now, shard_axis, list(map(lambda b: (b, b ^ frame_out), ra...  2.97 us
  transfers between devices with their start and end apart: 4, of which 1 were waited for; matrix products, arithmetic and copies ran while one was open for 8% of the time, Pallas kernels for 0%

profile of v1, /device:TPU:0, one launch (start us, length us, event | category | flops | bytes accessed | tf_op | source)
XLA Modules:
  0.0 118.2 jit_solution(14463454873200724479)
XLA Ops:
  6.5 3.0 %collective-permute-start.2 = (bf16[128,2048]{1,0:T(8,128)(2,1)}, bf16[128,2048]{1,0:T(8,128)(2,1)S(1)}, u32[]{:S(2)}, u32[]{:S(2)}) collective-permute-start(bf16[128,2048]{1,0:T(8,128)(2,1)} %param.7), channel_id=1, source_target_pairs={{0,1},{1,0},{2,3},{3,2},{4,5},{5,4},{6,7},{7,6},{8,9},{9,8},{10,11... | collective-permute-start | bytes 1572872 | tf_op jit(solution)/shard_map/ppermute | solution.py:101
  9.5 0.7 iota_compare_fusion.1
  10.2 1.1 copy.59
  11.4 1.2 %copy.58 = bf16[16,8,16,128]{3,2,1,0:T(8,128)(2,1)S(1)} copy(bf16[16,8,16,128]{3,1,2,0:T(8,128)(2,1)} %bitcast.143) | data formatting | bytes 1048576
  12.6 0.2 fusion.25
  12.9 0.2 fusion.27
  13.1 9.9 %all_gather.10 = bf16[2,16,16,128]{3,1,2,0:T(8,128)(2,1)S(1)} all-gather(bf16[2,8,16,128]{3,1,2,0:T(8,128)(2,1)S(1)} %pad_maximum_fusion.1), channel_id=1, replica_groups=mesh['seg'=16,'blk'=2] {'blk'}, dimensions={1}, use_global_device_ids=true | all-gather | bytes 196608 | tf_op jit(solution)/shard_map/all_gather | solution.py:130
  23.1 1.0 copy.23
  24.1 0.3 copy.54
  24.5 0.2 fusion.18
  24.7 0.3 fusion.21
  25.0 0.1 copy.57
  25.1 0.2 fusion.29
  25.3 0.4 fusion.43
  25.7 70.7 %all_gather.11 = bf16[2,32,16,128]{3,2,1,0:T(8,128)(2,1)S(1)} all-gather(bf16[2,1,16,128]{3,2,1,0:T(8,128)(2,1)S(1)} %pad_maximum_fusion.2), channel_id=1, replica_groups=mesh['seg'=16,'blk'=2] {'seg','blk'}, dimensions={1}, use_global_device_ids=true | all-gather | bytes 270336 | tf_op jit(solution)/shard_map/all_gather | solution.py:146
  96.4 0.2 fusion.35
  96.6 0.1 multiply_reduce_fusion.1
  96.8 0.2 fusion.57
  96.9 0.2 fusion.33
  97.4 0.1 broadcast_in_dim.103
  97.5 6.2 %collective-permute-done.1 = bf16[2,32,16,128]{3,1,2,0:T(8,128)(2,1)S(1)} collective-permute-done((bf16[2,32,16,128]{3,1,2,0:T(8,128)(2,1)S(1)}, bf16[2,32,16,128]{3,1,2,0:T(8,128)(2,1)S(1)}, u32[]{:S(2)}, u32[]{:S(2)}) %collective-permute-start.1) | collective-permute-done | bytes 262176 | tf_op jit(solution)/shard_map/ppermute | solution.py:15
  103.7 0.3 fusion.62
  104.0 0.2 fusion.38
  104.3 0.1 broadcast_in_dim.105
  104.4 0.2 fusion.6
  104.7 1.4 %copy.31 = f32[128,16,128]{0,2,1:T(8,128)} copy(f32[128,16,128]{2,1,0:T(8,128)S(1)} %bitcast.141) | data formatting | bytes 2097152 | tf_op jit(solution)/shard_map/jit(_where)/broadcast_in_dim | solution.py:71
  106.2 0.3 copy.53
  106.5 1.8 %multiply_reduce_fusion = (f32[16,128]{1,0:T(8,128)S(1)}, f32[16,128,256]{2,1,0:T(8,128)S(1)}) fusion(bf16[256,16,128]{0,2,1:T(8,128)(2,1)} %bitcast.150, bf16[128,2048]{1,0:T(8,128)(2,1)S(1)} %copy-done), kind=kOutput, calls=%fused_computation.1 | convolution fusion | flops 135264256 | bytes 3678208 | tf_op jit(solution)/shard_map/qhd,khd->hqk/dot_general | solution.py:45
  108.3 0.8 fusion.1
  109.1 0.1 add_add_fusion
  109.2 1.1 divide_convert_fusion
  110.3 1.0 copy.32
  (37 shorter events, 0.6 us)
Async XLA Ops:
  6.5 16.5 %copy-start.1 = (bf16[128,2048]{1,0:T(8,128)(2,1)S(1)}, bf16[128,2048]{1,0:T(8,128)(2,1)}, u32[]{:S(2)}) copy-start(bf16[128,2048]{1,0:T(8,128)(2,1)} %param.6) | copy-start | bytes 1572868
  6.5 99.9 %all-gather.2.cloned.1.call-start = ((), (), s32[]{:S(2)}) async-start(), calls=%async_computation | async-start | bytes 1572864 | tf_op jit(solution)/shard_map/all_gather | solution.py:111
  6.5 99.6 %collective-permute-start.2 = (bf16[128,2048]{1,0:T(8,128)(2,1)}, bf16[128,2048]{1,0:T(8,128)(2,1)S(1)}, u32[]{:S(2)}, u32[]{:S(2)}) collective-permute-start(bf16[128,2048]{1,0:T(8,128)(2,1)} %param.7), channel_id=1, source_target_pairs={{0,1},{1,0},{2,3},{3,2},{4,5},{5,4},{6,7},{7,6},{8,9},{9,8},{10,11... | collective-permute-start | bytes 1572872 | tf_op jit(solution)/shard_map/ppermute | solution.py:101
  11.4 12.7 %copy-start.2 = (bf16[128,2048]{1,0:T(8,128)(2,1)S(1)}, bf16[128,2048]{1,0:T(8,128)(2,1)}, u32[]{:S(2)}) copy-start(bf16[128,2048]{1,0:T(8,128)(2,1)} %param.7) | copy-start | bytes 1572868
  12.6 11.8 %copy-start.4 = (s32[16]{0:T(128)S(1)}, s32[16]{0:T(128)}, u32[]{:S(2)}) copy-start(s32[16]{0:T(128)} %param.9) | copy-start | bytes 196
  12.9 11.9 %copy-start = (bf16[128,2048]{1,0:T(8,128)(2,1)S(1)}, bf16[128,2048]{1,0:T(8,128)(2,1)}, u32[]{:S(2)}) copy-start(bf16[128,2048]{1,0:T(8,128)(2,1)} %param.5) | copy-start | bytes 1572868
  23.1 74.1 %collective-permute-start = (bf16[2,16,16,128]{3,1,2,0:T(8,128)(2,1)S(1)}, bf16[2,16,16,128]{3,1,2,0:T(8,128)(2,1)S(1)}, u32[]{:S(2)}, u32[]{:S(2)}) collective-permute-start(bf16[2,16,16,128]{3,1,2,0:T(8,128)(2,1)S(1)} %all_gather.10), channel_id=1, source_target_pairs={{0,2},{2,0},{4,6},{6,4},{8,10},{10,8},{12,14},{14,12},{16,18},{18,... | collective-permute-start | bytes 393224 | tf_op jit(solution)/shard_map/ppermute | solution.py:15
  97.2 6.4 %collective-permute-start.1 = (bf16[2,32,16,128]{3,1,2,0:T(8,128)(2,1)S(1)}, bf16[2,32,16,128]{3,1,2,0:T(8,128)(2,1)S(1)}, u32[]{:S(2)}, u32[]{:S(2)}) collective-permute-start(bf16[2,32,16,128]{3,1,2,0:T(8,128)(2,1)S(1)} %pad_maximum_fusion), channel_id=1, source_target_pairs={{0,4},{2,6},{4,0},{6,2},{8,12},{10,14},{12,8},{14,10},{16,20},{18,... | collective-permute-start | bytes 786440 | tf_op jit(solution)/shard_map/ppermute | solution.py:15
  106.5 2.7 %copy-start.3 = (f32[128,16,128]{0,2,1:T(8,128)S(1)}, f32[128,16,128]{0,2,1:T(8,128)}, u32[]{:S(2)}) copy-start(f32[128,16,128]{0,2,1:T(8,128)} %copy.31) | copy-start | bytes 3145732
Sparse Core Ops, SparseCore 0:
  24.2 24.0 all-gather.1
